TPU v7x, 128 devices: a whole 4x4x4 slice. The times are simulated.
128 devices in a mesh: pipe: 2 (over x_hi), tensor: 4 (over z), dp: 16 (over x_lo, y, core).
Axes of the slice: x: 4 (x_hi: 2, x_lo: 2; x = x_hi * 2 + x_lo), y: 4, z: 4, core: 2. Of those that a mesh axis runs over, the one named last changes fastest.
Arguments:
- tokens: bfloat16 [8192, 1024], P('dp', 'tensor'), may hold values from -6 to 6
- lengths: int32 [64, 4], P('dp'), may hold values from 1 to 85, 128 in all within a row
- ln_gain: bfloat16 [2, 2, 1024], P('pipe'), may hold values from 0.099609375 to 1.8984375
- ln_bias: bfloat16 [2, 2, 1024], P('pipe'), may hold values from -3 to 3
- joined_weight: bfloat16 [2, 1024, 3, 1024], P('pipe', None, None, 'tensor'), may hold values from -0.1875 to 0.1875
- joined_bias: bfloat16 [2, 3, 1024], P('pipe', None, 'tensor'), may hold values from -3 to 3
- dense_weight: bfloat16 [2, 1024, 1024], P('pipe', 'tensor'), may hold values from -0.5 to 0.5
- up_weight: bfloat16 [2, 1024, 4096], P('pipe', None, 'tensor'), may hold values from -0.1875 to 0.1875
- up_bias: bfloat16 [2, 4096], P('pipe', 'tensor'), may hold values from -3 to 3
- down_weight: bfloat16 [2, 4096, 1024], P('pipe', 'tensor'), may hold values from -0.09375 to 0.09375
- output_bias: bfloat16 [2, 2, 1024], P('pipe'), may hold values from -3 to 3
- cotangent: bfloat16 [8192, 1024], P('dp', 'tensor'), may hold values from -6 to 6
Outputs:
- section_out: bfloat16 [2, 8192, 1024], P('pipe', 'dp', 'tensor')
- input_grad: bfloat16 [2, 8192, 1024], P('pipe', 'dp', 'tensor')
- grad_ln_gain: float32 [2, 2, 1024], P('pipe')
- grad_ln_bias: float32 [2, 2, 1024], P('pipe')
- grad_joined: float32 [2, 1024, 3, 1024], P('pipe', None, None, 'tensor')
- grad_joined_bias: float32 [2, 3, 1024], P('pipe', None, 'tensor')
- grad_dense: float32 [2, 1024, 1024], P('pipe', 'tensor')
- grad_up: float32 [2, 1024, 4096], P('pipe', None, 'tensor')
- grad_up_bias: float32 [2, 4096], P('pipe', 'tensor')
- grad_down: float32 [2, 4096, 1024], P('pipe', 'tensor')
- grad_output_bias: float32 [2, 2, 1024], P('pipe')
Inputs may be any that keep to these rules, and one draw needn't show every extreme that they name: Row b gives, in order, the lengths of the 4 sequences that fill block b (tokens b * 128 to (b + 1) * 128 - 1); every row sums to 128.
All inputs are finite; a program needn't handle non-finite values.
Results may differ from a plain program's by a relative error of at most 0.035.
Values may be sent and summed in bfloat16 or wider, within the bound.
No kernel may reach another device: no remote copies, remote signals or barrier semaphores. Data moves between devices by JAX's collectives and lax.ppermute only.
A program may use at most 192 MiB of HBM per device.

v0:
```python
import jax
import jax.numpy as jnp
from jax import lax
from jax.sharding import PartitionSpec as P

HD = 64
ROT = 16
MB = 128
NMB = 4


EPSILON = 1e-05
MASKED = -1e30


def passed_along(x, axis, by):
    peers = lax.axis_size(axis)
    pairs = [(i, i + by) for i in range(peers) if 0 <= i + by < peers]
    return lax.ppermute(x, axis, pairs)


def as_sent(x):
    return jax.tree.map(lambda a: a.astype(jnp.bfloat16) if a.dtype == jnp.float32 else a, x)


def positions(lengths, block_rows):
    seq_count = lengths.shape[1]
    counter = jnp.arange(seq_count, dtype=jnp.int32)
    lower_tri = (counter[:, None] >= counter[None, :]).astype(jnp.int32)
    seg_ends = jnp.sum(lengths[:, None, :] * lower_tri[None, :, :], axis=2)
    starts = seg_ends - lengths
    row_index = jnp.arange(block_rows, dtype=jnp.int32)
    segment = jnp.sum((row_index[None, :, None] >= seg_ends[:, None, :]).astype(jnp.int32), axis=2)
    member = (segment[:, :, None] == counter[None, None, :]).astype(jnp.int32)
    place = row_index[None, :] - jnp.sum(member * starts[:, None, :], axis=2)
    return (segment, place)


def rotary(place):
    half_rot = ROT // 2
    inv_freq = jnp.power(10000.0, -2.0 * jnp.arange(half_rot, dtype=jnp.float32) / ROT)
    angles = place.astype(jnp.float32)[..., None] * inv_freq
    return (jnp.cos(angles), jnp.sin(angles))


def rotate(heads_in, cosv, sinv):
    half_rot = ROT // 2
    first_half = heads_in[..., :half_rot]
    second_half = heads_in[..., half_rot:ROT]
    cos_rows = cosv[:, None, :]
    sin_rows = sinv[:, None, :]
    return jnp.concatenate(
        [
            first_half * cos_rows - second_half * sin_rows,
            second_half * cos_rows + first_half * sin_rows,
            heads_in[..., ROT:],
        ],
        axis=-1,
    )


def rotate_back(heads_in, cosv, sinv):
    half_rot = ROT // 2
    first_half = heads_in[..., :half_rot]
    second_half = heads_in[..., half_rot:ROT]
    cos_rows = cosv[:, None, :]
    sin_rows = sinv[:, None, :]
    return jnp.concatenate(
        [
            first_half * cos_rows + second_half * sin_rows,
            second_half * cos_rows - first_half * sin_rows,
            heads_in[..., ROT:],
        ],
        axis=-1,
    )


def exact_gelu(values):
    return jax.nn.gelu(values, approximate=False)


def allowed_keys(segment):
    row_index = jnp.arange(segment.shape[0], dtype=jnp.int32)
    return (segment[:, None] == segment[None, :]) & (row_index[None, :] <= row_index[:, None])


def contract_rows(left, right):
    return lax.dot_general(
        left, right, (((0,), (0,)), ((), ())), preferred_element_type=jnp.float32
    )


def contract_cols(left, right):
    return lax.dot_general(
        left, right, (((1,), (1,)), ((), ())), preferred_element_type=jnp.float32
    )


def per_device(
    tokens,
    lengths,
    ln_gain,
    ln_bias,
    joined_weight,
    joined_bias,
    dense_weight,
    up_weight,
    up_bias,
    down_weight,
    output_bias,
    cotangent,
):
    leading = lax.axis_index("pipe") == 0
    model_width = joined_weight.shape[1]
    local_width = joined_weight.shape[3]
    local_heads = local_width // HD
    hidden_local = up_weight.shape[2]
    quarter = tokens.shape[1]
    score_scale = HD ** (-0.5)
    ln_gains = ln_gain[0].astype(jnp.float32)
    ln_shifts = ln_bias[0].astype(jnp.float32)
    joined_mat = joined_weight[0].reshape(model_width, 3 * local_width)
    joined_add = joined_bias[0].astype(jnp.float32).reshape(3 * local_width)
    dense_mat = dense_weight[0]
    up_mat = up_weight[0]
    up_add = up_bias[0].astype(jnp.float32)
    down_mat = down_weight[0]
    bias_sum = output_bias[0, 0].astype(jnp.float32) + output_bias[0, 1].astype(jnp.float32)
    input_rows, output_grads = (
        lax.all_gather(tokens, "tensor", axis=1, tiled=True),
        lax.all_gather(cotangent, "tensor", axis=1, tiled=True),
    )
    segment_all, place_all = positions(lengths, MB)
    cos_all, sin_all = rotary(place_all)

    def pick(early_val, late_val):
        return jax.tree.map(
            lambda upper_val, lower_val: jnp.where(leading, upper_val, lower_val),
            early_val,
            late_val,
        )

    received = jnp.zeros((MB, model_width), jnp.bfloat16)
    tick_outputs = []
    tick_stored = []
    for section_tick in range(NMB + 1):
        early_block = min(section_tick, NMB - 1)
        late_block = max(section_tick - 1, 0)
        block_rows = jnp.where(
            leading, input_rows[early_block * MB : (early_block + 1) * MB], received
        )
        segment, cosv, sinv = pick(
            (segment_all[early_block], cos_all[early_block], sin_all[early_block]),
            (segment_all[late_block], cos_all[late_block], sin_all[late_block]),
        )
        inputs = block_rows.astype(jnp.float32)
        row_mean = jnp.mean(inputs, axis=1, keepdims=True)
        centred = inputs - row_mean
        forward_inv_scale = lax.rsqrt(jnp.mean(centred * centred, axis=1, keepdims=True) + EPSILON)
        forward_normed = centred * forward_inv_scale
        forward_h_attn = (forward_normed * ln_gains[0] + ln_shifts[0]).astype(jnp.bfloat16)
        forward_h_mlp = (forward_normed * ln_gains[1] + ln_shifts[1]).astype(jnp.bfloat16)
        joined_proj = (
            jnp.dot(forward_h_attn, joined_mat, preferred_element_type=jnp.float32) + joined_add
        )
        forward_block_len = block_rows.shape[0]
        forward_queries = rotate(
            joined_proj[:, :local_width].reshape(forward_block_len, local_heads, HD), cosv, sinv
        ).astype(jnp.bfloat16)
        forward_keys_rot = rotate(
            joined_proj[:, local_width : 2 * local_width].reshape(
                forward_block_len, local_heads, HD
            ),
            cosv,
            sinv,
        ).astype(jnp.bfloat16)
        forward_values = (
            joined_proj[:, 2 * local_width :]
            .reshape(forward_block_len, local_heads, HD)
            .astype(jnp.bfloat16)
        )
        forward_scores = (
            jnp.einsum(
                "qhd,khd->hqk",
                forward_queries,
                forward_keys_rot,
                preferred_element_type=jnp.float32,
            )
            * score_scale
        )
        forward_scores = jnp.where(allowed_keys(segment)[None], forward_scores, MASKED)
        row_top = jnp.max(forward_scores, axis=2, keepdims=True)
        exponent = jnp.exp(forward_scores - row_top)
        row_total = jnp.sum(exponent, axis=2, keepdims=True)
        forward_log_total = row_top + jnp.log(row_total)
        weights_low = (exponent / row_total).astype(jnp.bfloat16)
        forward_context = jnp.einsum(
            "hqk,khd->qhd", weights_low, forward_values, preferred_element_type=jnp.float32
        )
        forward_context = forward_context.reshape(forward_block_len, local_width).astype(
            jnp.bfloat16
        )
        forward_up_proj = (
            jnp.dot(forward_h_mlp, up_mat, preferred_element_type=jnp.float32) + up_add
        )
        forward_activated = exact_gelu(forward_up_proj).astype(jnp.bfloat16)
        partial_value = jnp.dot(forward_context, dense_mat, preferred_element_type=jnp.float32)
        partial_value = partial_value + jnp.dot(
            forward_activated, down_mat, preferred_element_type=jnp.float32
        )
        branches = lax.psum(partial_value.astype(jnp.bfloat16), "tensor").astype(jnp.float32)
        result = inputs + branches + bias_sum
        forward_stored = (
            forward_normed,
            forward_inv_scale,
            forward_h_attn,
            forward_h_mlp,
            forward_queries,
            forward_keys_rot,
            forward_values,
            forward_log_total,
            forward_context,
            forward_up_proj,
            forward_activated,
        )
        result, stored = (result, forward_stored)
        result_low = result.astype(jnp.bfloat16)
        tick_outputs.append(result_low)
        tick_stored.append((stored, segment, cosv, sinv))
        if section_tick < NMB:
            received = passed_along(result_low, "pipe", 1)
    column_start = lax.axis_index("tensor") * quarter
    section_rows = jnp.concatenate(
        [jnp.where(leading, tick_outputs[block], tick_outputs[block + 1]) for block in range(NMB)],
        axis=0,
    )
    section_out = lax.dynamic_slice_in_dim(section_rows, column_start, quarter, 1)[None]
    returned = jnp.zeros((MB, model_width), jnp.bfloat16)
    tick_grads = []
    totals = None
    for section_tick in range(NMB + 1):
        own_block = min(section_tick, NMB - 1)
        late_tick = max(section_tick - 1, 0)
        upper_tick = min(section_tick + 1, NMB)
        from_output = output_grads[own_block * MB : (own_block + 1) * MB]
        if section_tick == NMB:
            from_output = jnp.zeros_like(from_output)
        grad_rows = jnp.where(leading, returned, from_output)
        stored, segment, cosv, sinv = pick(tick_stored[late_tick], tick_stored[upper_tick])
        (
            normed,
            inv_scale,
            h_attn,
            h_mlp,
            queries,
            keys_rot,
            values,
            log_total,
            context,
            up_proj,
            activated,
        ) = stored
        block_len = grad_rows.shape[0]
        grad_wide = grad_rows.astype(jnp.float32)
        column_sum = jnp.sum(grad_wide, axis=0)
        backward_grad_dense = contract_rows(context, grad_rows)
        backward_grad_down = contract_rows(activated, grad_rows)
        d_context = contract_cols(grad_rows, dense_mat).astype(jnp.bfloat16)
        d_act = contract_cols(grad_rows, down_mat)
        unused, slope_back = jax.vjp(exact_gelu, up_proj)
        d_up = slope_back(d_act)[0].astype(jnp.bfloat16)
        grad_up_add = jnp.sum(d_up.astype(jnp.float32), axis=0)
        backward_grad_up = contract_rows(h_mlp, d_up)
        d_hmlp = contract_cols(d_up, up_mat)
        scores = (
            jnp.einsum("qhd,khd->hqk", queries, keys_rot, preferred_element_type=jnp.float32)
            * score_scale
        )
        scores = jnp.where(allowed_keys(segment)[None], scores, MASKED)
        weights_soft = jnp.exp(scores - log_total)
        d_context3 = d_context.reshape(block_len, local_heads, HD)
        d_values = jnp.einsum(
            "hqk,qhd->khd",
            weights_soft.astype(jnp.bfloat16),
            d_context3,
            preferred_element_type=jnp.float32,
        ).astype(jnp.bfloat16)
        d_weights = jnp.einsum(
            "qhd,khd->hqk", d_context3, values, preferred_element_type=jnp.float32
        )
        row_delta = jnp.sum(weights_soft * d_weights, axis=2, keepdims=True)
        d_scores = (weights_soft * (d_weights - row_delta)).astype(jnp.bfloat16)
        d_queries = (
            jnp.einsum("hqk,khd->qhd", d_scores, keys_rot, preferred_element_type=jnp.float32)
            * score_scale
        )
        d_keys = (
            jnp.einsum("hqk,qhd->khd", d_scores, queries, preferred_element_type=jnp.float32)
            * score_scale
        )
        d_queries = (
            rotate_back(d_queries, cosv, sinv).reshape(block_len, local_width).astype(jnp.bfloat16)
        )
        d_keys = (
            rotate_back(d_keys, cosv, sinv).reshape(block_len, local_width).astype(jnp.bfloat16)
        )
        d_joined = jnp.concatenate(
            [d_queries, d_keys, d_values.reshape(block_len, local_width)], axis=1
        )
        grad_joined_add = jnp.sum(d_joined.astype(jnp.float32), axis=0)
        backward_grad_joined = contract_rows(h_attn, d_joined)
        d_hattn = contract_cols(d_joined, joined_mat)
        d_hattn, d_hmlp = (
            lax.psum(d_hattn.astype(jnp.bfloat16), "tensor").astype(jnp.float32),
            lax.psum(d_hmlp.astype(jnp.bfloat16), "tensor").astype(jnp.float32),
        )
        grad_gains = jnp.concatenate(
            [jnp.sum(d_hattn * normed, axis=0), jnp.sum(d_hmlp * normed, axis=0)]
        )
        grad_shifts = jnp.concatenate([jnp.sum(d_hattn, axis=0), jnp.sum(d_hmlp, axis=0)])
        d_norm = d_hattn * ln_gains[0] + d_hmlp * ln_gains[1]
        grad_input = grad_wide + inv_scale * (
            d_norm
            - jnp.mean(d_norm, axis=1, keepdims=True)
            - normed * jnp.mean(d_norm * normed, axis=1, keepdims=True)
        )
        small_terms = jnp.concatenate(
            [grad_gains, grad_shifts, column_sum, column_sum, grad_joined_add, grad_up_add]
        )
        terms = (
            backward_grad_joined[None],
            backward_grad_dense[None],
            backward_grad_up[None],
            backward_grad_down[None],
            small_terms[None],
        )
        grad_input, terms = (grad_input, terms)
        grad_low = grad_input.astype(jnp.bfloat16)
        tick_grads.append(grad_low)
        if totals is None:
            totals = terms
        else:
            totals = jax.tree.map(lambda older, newer: older + newer, totals, terms)
        if section_tick < NMB:
            returned = passed_along(grad_low, "pipe", -1)
    totals = jax.tree.map(
        lambda part: part.astype(jnp.float32),
        lax.psum_scatter(as_sent(totals), "dp", scatter_dimension=1, tiled=True),
    )
    summed = jax.tree.map(
        lambda part, own: part.astype(own.dtype),
        lax.all_gather(as_sent(totals), "dp", axis=1, tiled=True),
        totals,
    )
    grad_rows_all = jnp.concatenate(
        [jnp.where(leading, tick_grads[block + 1], tick_grads[block]) for block in range(NMB)],
        axis=0,
    )
    input_grad = lax.dynamic_slice_in_dim(grad_rows_all, column_start, quarter, 1)[None]
    grad_joined = summed[0].reshape(1, model_width, 3, local_width)
    grad_dense = summed[1]
    grad_up = summed[2]
    grad_down = summed[3]
    small_sum = summed[4][0]
    offset = 0
    grad_ln_gain = small_sum[offset : offset + 2 * model_width].reshape(1, 2, model_width)
    offset = offset + 2 * model_width
    grad_ln_bias = small_sum[offset : offset + 2 * model_width].reshape(1, 2, model_width)
    offset = offset + 2 * model_width
    grad_output_bias = small_sum[offset : offset + 2 * model_width].reshape(1, 2, model_width)
    offset = offset + 2 * model_width
    grad_joined_bias = small_sum[offset : offset + 3 * local_width].reshape(1, 3, local_width)
    offset = offset + 3 * local_width
    grad_up_bias = small_sum[offset : offset + hidden_local].reshape(1, hidden_local)
    return (
        section_out,
        input_grad,
        grad_ln_gain,
        grad_ln_bias,
        grad_joined,
        grad_joined_bias,
        grad_dense,
        grad_up,
        grad_up_bias,
        grad_down,
        grad_output_bias,
    )


def solution(mesh):
    placed = (
        P("dp", "tensor"),
        P("dp", None),
        P("pipe", None, None),
        P("pipe", None, None),
        P("pipe", None, None, "tensor"),
        P("pipe", None, "tensor"),
        P("pipe", "tensor", None),
        P("pipe", None, "tensor"),
        P("pipe", "tensor"),
        P("pipe", "tensor", None),
        P("pipe", None, None),
        P("dp", "tensor"),
    )
    return jax.shard_map(
        per_device,
        mesh=mesh,
        in_specs=placed,
        out_specs=(
            P("pipe", "dp", "tensor"),
            P("pipe", "dp", "tensor"),
            P("pipe", None, None),
            P("pipe", None, None),
            P("pipe", None, None, "tensor"),
            P("pipe", None, "tensor"),
            P("pipe", "tensor", None),
            P("pipe", None, "tensor"),
            P("pipe", "tensor"),
            P("pipe", "tensor", None),
            P("pipe", None, None),
        ),
        check_vma=False,
    )
```

profile of v0, /device:TPU:0, one launch (start us, length us, event | category | flops | bytes accessed | tf_op | source)
XLA Modules:
  0.0 982.8 jit_solution(12664540825030383722)
XLA Ops:
  17.0 21.3 %all-gather.6.cloned.1.call-done = bf16[512,1024]{1,0:T(8,128)(2,1)} async-done(((bf16[512,256]{1,0:T(8,128)(2,1)}), bf16[512,1024]{1,0:T(8,128)(2,1)}) %all-gather.6.cloned.1.call-update) | async-done | bytes 1048592 | tf_op jit(solution)/shard_map/all_gather | solution.py:130
  60.1 33.5 %all-reduce.13.cloned.1.call-done = bf16[128,1024]{1,0:T(8,128)(2,1)} async-done(((bf16[128,1024]{1,0:T(8,128)(2,1)}), bf16[128,1024]{1,0:T(8,128)(2,1)}) %all-reduce.13.cloned.1.call-update) | async-done | bytes 262160 | tf_op jit(solution)/shard_map/psum | solution.py:211
  94.8 5.1 collective-permute-start
  100.5 21.3 %all-gather.8.cloned.1.call-done = bf16[512,1024]{1,0:T(8,128)(2,1)} async-done(((bf16[512,256]{1,0:T(8,128)(2,1)}), bf16[512,1024]{1,0:T(8,128)(2,1)}) %all-gather.8.cloned.1.call-update) | async-done | bytes 1048592 | tf_op jit(solution)/shard_map/all_gather | solution.py:131
  149.3 43.0 %all-reduce.23.cloned.1.call-done = (bf16[128,1024]{1,0:T(8,128)(2,1)}, bf16[128,1024]{1,0:T(8,128)(2,1)}, bf16[128,1024]{1,0:T(8,128)(2,1)}) async-done(((bf16[128,1024]{1,0:T(8,128)(2,1)}, bf16[128,1024]{1,0:T(8,128)(2,1)}, bf16[128,1024]{1,0:T(8,128)(2,1)}), (bf16[128,1024]{1,0:T(8,128)(2,1)}, bf16[128,1024]{1,0:T(8,128)(2,1)}, bf16[128,1024]{1,0:T(8,128)(2,1)})) %all-reduce.23.cloned.1.call-update) | async-done | bytes 786448 | tf_op jit(solution)/shard_map/psum | solution.py:315
  194.2 5.0 collective-permute-start.1
  199.2 3.9 fusion.386
  244.2 5.4 fusion.377
  249.6 36.9 %all-reduce.21.cloned.1.call-done = (bf16[128,1024]{1,0:T(8,128)(2,1)}, bf16[128,1024]{1,0:T(8,128)(2,1)}, bf16[128,1024]{1,0:T(8,128)(2,1)}) async-done(((bf16[128,1024]{1,0:T(8,128)(2,1)}, bf16[128,1024]{1,0:T(8,128)(2,1)}, bf16[128,1024]{1,0:T(8,128)(2,1)}), (bf16[128,1024]{1,0:T(8,128)(2,1)}, bf16[128,1024]{1,0:T(8,128)(2,1)}, bf16[128,1024]{1,0:T(8,128)(2,1)})) %all-reduce.21.cloned.1.call-update) | async-done | bytes 786448 | tf_op jit(solution)/shard_map/psum | solution.py:315
  288.5 4.8 collective-permute-start.2
  293.4 3.8 collective-permute-done.2
  344.0 6.1 fusion.375
  350.1 35.3 %all-reduce.19.cloned.1.call-done = (bf16[128,1024]{1,0:T(8,128)(2,1)}, bf16[128,1024]{1,0:T(8,128)(2,1)}, bf16[128,1024]{1,0:T(8,128)(2,1)}) async-done(((bf16[128,1024]{1,0:T(8,128)(2,1)}, bf16[128,1024]{1,0:T(8,128)(2,1)}, bf16[128,1024]{1,0:T(8,128)(2,1)}), (bf16[128,1024]{1,0:T(8,128)(2,1)}, bf16[128,1024]{1,0:T(8,128)(2,1)}, bf16[128,1024]{1,0:T(8,128)(2,1)})) %all-reduce.19.cloned.1.call-update) | async-done | bytes 786448 | tf_op jit(solution)/shard_map/psum | solution.py:315
  390.3 5.0 collective-permute-start.3
  402.5 5.2 collective-permute-done.6
  437.9 36.2 %all-reduce.17.cloned.1.call-done = (bf16[128,1024]{1,0:T(8,128)(2,1)}, bf16[128,1024]{1,0:T(8,128)(2,1)}) async-done(((bf16[128,1024]{1,0:T(8,128)(2,1)}, bf16[128,1024]{1,0:T(8,128)(2,1)}), (bf16[128,1024]{1,0:T(8,128)(2,1)}, bf16[128,1024]{1,0:T(8,128)(2,1)})) %all-reduce.17.cloned.1.call-update) | async-done | bytes 524304 | tf_op jit(solution)/shard_map/psum | solution.py:315
  482.5 6.0 collective-permute-done.7
  503.4 5.3 fusion.42
  509.0 4.1 fusion.384
  520.2 4.2 fusion
  556.9 53.8 %reduce-scatter.8.cloned.1.call-done = bf16[1,64,768]{2,1,0:T(8,128)(2,1)} async-done(((bf16[1,1024,768]{2,1,0:T(8,128)(2,1)}), bf16[1,64,768]{2,1,0:T(8,128)(2,1)}) %reduce-scatter.8.cloned.1.call-update) | async-done | bytes 98320 | tf_op jit(solution)/shard_map/reduce_scatter | solution.py:348
  610.8 64.2 %reduce-scatter.14.cloned.1.call-done = bf16[1,64,1024]{2,1,0:T(8,128)(2,1)} async-done(((bf16[1,1024,1024]{2,1,0:T(8,128)(2,1)}), bf16[1,64,1024]{2,1,0:T(8,128)(2,1)}) %reduce-scatter.14.cloned.1.call-update) | async-done | bytes 131088 | tf_op jit(solution)/shard_map/reduce_scatter | solution.py:348
  675.0 64.8 %reduce-scatter.12.cloned.1.call-done = bf16[1,64,1024]{2,1,0:T(8,128)(2,1)} async-done(((bf16[1,1024,1024]{2,1,0:T(8,128)(2,1)}), bf16[1,64,1024]{2,1,0:T(8,128)(2,1)}) %reduce-scatter.12.cloned.1.call-update) | async-done | bytes 131088 | tf_op jit(solution)/shard_map/reduce_scatter | solution.py:348
  743.9 60.7 %reduce-scatter.16.cloned.1.call-done = bf16[496,1]{1,0:T(8,128)(2,1)} async-done(((bf16[7936,1]{1,0:T(8,128)(2,1)}), bf16[496,1]{1,0:T(8,128)(2,1)}) %reduce-scatter.16.cloned.1.call-update) | async-done | bytes 1008
  805.9 53.1 %all-reduce = bf16[7936]{0:T(1024)(128)(2,1)S(1)} all-reduce(bf16[7936]{0:T(1024)(128)(2,1)S(1)} %dynamic-update-slice), channel_id=1, replica_groups=mesh['pipe'=2,'tensor'=4,'dp'=16] {'dp'}, use_global_device_ids=true, to_apply=%add | all-reduce | flops 7936 | bytes 31744
  862.1 4.7 reduce-scatter.10.cloned.1.call-done
  866.8 18.3 %all_gather.25 = bf16[1,256,1024]{2,1,0:T(8,128)(2,1)S(1)} all-gather(bf16[1,16,1024]{2,1,0:T(8,128)(2,1)} %reduce-scatter.10.cloned.1.call-done), channel_id=1, replica_groups=mesh['pipe'=2,'tensor'=4,'dp'=16] {'dp'}, dimensions={1}, use_global_device_ids=true | all-gather | bytes 557056 | tf_op jit(solution)/shard_map/all_gather | solution.py:352
  886.2 14.2 %all-gather.10.cloned.1.call-done = bf16[1,1024,768]{2,1,0:T(8,128)(2,1)} async-done(((bf16[1,64,768]{2,1,0:T(8,128)(2,1)}), bf16[1,1024,768]{2,1,0:T(8,128)(2,1)}) %all-gather.10.cloned.1.call-update) | async-done | bytes 1572880 | tf_op jit(solution)/shard_map/all_gather | solution.py:352
  907.0 29.0 %all-gather.14.cloned.1.call-done = bf16[1,1024,1024]{2,1,0:T(8,128)(2,1)} async-done(((bf16[1,64,1024]{2,1,0:T(8,128)(2,1)}), bf16[1,1024,1024]{2,1,0:T(8,128)(2,1)}) %all-gather.14.cloned.1.call-update) | async-done | bytes 2097168 | tf_op jit(solution)/shard_map/all_gather | solution.py:352
  936.0 4.1 convert_element_type.728
  940.1 31.6 %all-gather.12.cloned.1.call-done = bf16[1,1024,1024]{2,1,0:T(8,128)(2,1)} async-done(((bf16[1,64,1024]{2,1,0:T(8,128)(2,1)}), bf16[1,1024,1024]{2,1,0:T(8,128)(2,1)}) %all-gather.12.cloned.1.call-update) | async-done | bytes 2097168 | tf_op jit(solution)/shard_map/all_gather | solution.py:352
  971.7 4.1 convert_element_type.725
  (1057 shorter events, 268.8 us)
Async XLA Ops:
  7.2 31.1 %all-gather.6.cloned.1.call-start = ((), (), s32[]{:S(2)}) async-start(), calls=%async_computation.5 | async-start | bytes 1310720 | tf_op jit(solution)/shard_map/all_gather | solution.py:130
  7.9 85.7 %all-reduce.13.cloned.1.call-start = ((), (), s32[]{:S(2)}) async-start(), calls=%async_computation.6 | async-start | bytes 524288 | tf_op jit(solution)/shard_map/psum | solution.py:211
  50.7 71.1 %all-gather.8.cloned.1.call-start = ((), (), s32[]{:S(2)}) async-start(), calls=%async_computation.7 | async-start | bytes 1310720 | tf_op jit(solution)/shard_map/all_gather | solution.py:131
  51.5 140.9 %all-reduce.23.cloned.1.call-start = ((), (), s32[]{:S(2)}) async-start(), calls=%async_computation.20 | async-start | bytes 1572864 | tf_op jit(solution)/shard_map/psum | solution.py:315
  94.8 28.5 %collective-permute-start = (bf16[128,1024]{1,0:T(8,128)(2,1)S(1)}, bf16[128,1024]{1,0:T(8,128)(2,1)S(1)}, u32[]{:S(2)}, u32[]{:S(2)}) collective-permute-start(bf16[128,1024]{1,0:T(8,128)(2,1)S(1)} %fusion.193), channel_id=1, source_target_pairs={{0,64},{1,65},{2,66},{3,67},{4,68},{5,69},{6,70},{7,71},{8,72},{9,... | collective-permute-start | bytes 786440 | tf_op jit(solution)/shard_map/ppermute | solution.py:19
  146.5 140.0 %all-reduce.21.cloned.1.call-start = ((), (), s32[]{:S(2)}) async-start(), calls=%async_computation.19 | async-start | bytes 1572864 | tf_op jit(solution)/shard_map/psum | solution.py:315
  194.2 8.9 collective-permute-start.1
  216.1 9.9 %collective-permute-start.4 = (bf16[128,1024]{1,0:T(8,128)(2,1)S(1)}, bf16[128,1024]{1,0:T(8,128)(2,1)}, u32[]{:S(2)}, u32[]{:S(2)}) collective-permute-start(bf16[128,1024]{1,0:T(8,128)(2,1)S(1)} %fusion.187), channel_id=1, source_target_pairs={{64,0},{65,1},{66,2},{67,3},{68,4},{69,5},{70,6},{71,7},{72,8},{73... | collective-permute-start | bytes 786440 | tf_op jit(solution)/shard_map/ppermute | solution.py:19
  239.8 145.6 %all-reduce.19.cloned.1.call-start = ((), (), s32[]{:S(2)}) async-start(), calls=%async_computation.18 | async-start | bytes 1572864 | tf_op jit(solution)/shard_map/psum | solution.py:315
  288.5 8.7 collective-permute-start.2
  314.3 10.1 %collective-permute-start.5 = (bf16[128,1024]{1,0:T(8,128)(2,1)}, bf16[128,1024]{1,0:T(8,128)(2,1)}, u32[]{:S(2)}, u32[]{:S(2)}) collective-permute-start(bf16[128,1024]{1,0:T(8,128)(2,1)} %get-tuple-element.113), channel_id=1, source_target_pairs={{64,0},{65,1},{66,2},{67,3},{68,4},{69,5},{70,6},{71,7},{72,8},{73... | collective-permute-start | bytes 786440 | tf_op jit(solution)/shard_map/ppermute | solution.py:19
  339.8 92.5 %copy-start.70 = (bf16[128,4,64]{0,2,1:T(8,128)(2,1)}, bf16[128,4,64]{0,2,1:T(8,128)(2,1)S(1)}, u32[]{:S(2)}) copy-start(bf16[128,4,64]{0,2,1:T(8,128)(2,1)S(1)} %pad_maximum_fusion.19) | copy-start | bytes 196612
  341.1 133.0 %all-reduce.17.cloned.1.call-start = ((), (), s32[]{:S(2)}) async-start(), calls=%async_computation.17 | async-start | bytes 1048576 | tf_op jit(solution)/shard_map/psum | solution.py:315
  390.3 9.2 collective-permute-start.3
  397.9 9.9 %collective-permute-start.6 = (bf16[128,1024]{1,0:T(8,128)(2,1)S(1)}, bf16[128,1024]{1,0:T(8,128)(2,1)S(1)}, u32[]{:S(2)}, u32[]{:S(2)}) collective-permute-start(bf16[128,1024]{1,0:T(8,128)(2,1)S(1)} %get-tuple-element.111), channel_id=1, source_target_pairs={{64,0},{65,1},{66,2},{67,3},{68,4},{69,5},{70,6},{71,7},{72,8},{73... | collective-permute-start | bytes 786440 | tf_op jit(solution)/shard_map/ppermute | solution.py:19
  432.3 117.8 %all-reduce.15.cloned.1.call-start = ((), (), s32[]{:S(2)}) async-start(), calls=%async_computation.16 | async-start | bytes 1572864 | tf_op jit(solution)/shard_map/psum | solution.py:315
  478.6 9.9 %collective-permute-start.7 = (bf16[128,1024]{1,0:T(8,128)(2,1)S(1)}, bf16[128,1024]{1,0:T(8,128)(2,1)S(1)}, u32[]{:S(2)}, u32[]{:S(2)}) collective-permute-start(bf16[128,1024]{1,0:T(8,128)(2,1)S(1)} %get-tuple-element.109), channel_id=1, source_target_pairs={{64,0},{65,1},{66,2},{67,3},{68,4},{69,5},{70,6},{71,7},{72,8},{73... | collective-permute-start | bytes 786440 | tf_op jit(solution)/shard_map/ppermute | solution.py:19
  501.3 109.4 %reduce-scatter.8.cloned.1.call-start = ((), (), s32[]{:S(2)}) async-start(), calls=%async_computation.8 | async-start | bytes 1671168 | tf_op jit(solution)/shard_map/reduce_scatter | solution.py:348
  508.7 166.3 %reduce-scatter.14.cloned.1.call-start = ((), (), s32[]{:S(2)}) async-start(), calls=%async_computation.13 | async-start | bytes 2228224 | tf_op jit(solution)/shard_map/reduce_scatter | solution.py:348
  524.5 215.4 %reduce-scatter.12.cloned.1.call-start = ((), (), s32[]{:S(2)}) async-start(), calls=%async_computation.11 | async-start | bytes 2228224 | tf_op jit(solution)/shard_map/reduce_scatter | solution.py:348
  547.9 256.7 %reduce-scatter.16.cloned.1.call-start = ((), (), s32[]{:S(2)}) async-start(), calls=%async_computation.15 | async-start | bytes 2158592
  553.7 313.1 %reduce-scatter.10.cloned.1.call-start = ((), (), s32[]{:S(2)}) async-start(), calls=%async_computation.10 | async-start | bytes 557056 | tf_op jit(solution)/shard_map/reduce_scatter | solution.py:348
  553.8 186.1 %copy-start.343 = (u32[128]{0:T(128)S(1)}, u32[128]{0:T(128)}, u32[]{:S(2)}) copy-start(u32[128]{0:T(128)} %constant.134) | copy-start | bytes 1540
  553.8 187.4 %copy-start.48 = (bf16[128,1024]{1,0:T(8,128)(2,1)S(1)}, bf16[128,1024]{1,0:T(8,128)(2,1)}, u32[]{:S(2)}) copy-start(bf16[128,1024]{1,0:T(8,128)(2,1)} %copy-done.47) | copy-start | bytes 786436
  553.8 187.4 %copy-start.121 = (f32[1,1,1024]{2,1,0:T(1,128)S(1)}, f32[1,1,1024]{2,1,0:T(1,128)}, u32[]{:S(2)}) copy-start(f32[1,1,1024]{2,1,0:T(1,128)} %copy-done.119) | copy-start | bytes 12292
  553.8 187.4 %copy-start.151 = (f32[128]{0:T(128)S(1)}, f32[128]{0:T(128)}, u32[]{:S(2)}) copy-start(f32[128]{0:T(128)} %copy-done.148) | copy-start | bytes 1540
  553.9 187.4 %copy-start.164 = (f32[128]{0:T(128)S(1)}, f32[128]{0:T(128)}, u32[]{:S(2)}) copy-start(f32[128]{0:T(128)} %copy-done.158) | copy-start | bytes 1540
  553.9 187.4 %copy-start.322 = (f32[128]{0:T(128)S(1)}, f32[128]{0:T(128)}, u32[]{:S(2)}) copy-start(f32[128]{0:T(128)} %get-tuple-element.276) | copy-start | bytes 1540
  556.9 186.1 %copy-start.62 = (bf16[128,1024]{1,0:T(8,128)(2,1)S(1)}, bf16[128,1024]{1,0:T(8,128)(2,1)}, u32[]{:S(2)}) copy-start(bf16[128,1024]{1,0:T(8,128)(2,1)} %get-tuple-element.144) | copy-start | bytes 786436
  556.9 343.5 %all-gather.10.cloned.1.call-start = ((), (), s32[]{:S(2)}) async-start(), calls=%async_computation.9 | async-start | bytes 1671168 | tf_op jit(solution)/shard_map/all_gather | solution.py:352
  610.7 325.3 %all-gather.14.cloned.1.call-start = ((), (), s32[]{:S(2)}) async-start(), calls=%async_computation.14 | async-start | bytes 2228224 | tf_op jit(solution)/shard_map/all_gather | solution.py:352
  675.0 296.7 %all-gather.12.cloned.1.call-start = ((), (), s32[]{:S(2)}) async-start(), calls=%async_computation.12 | async-start | bytes 2228224 | tf_op jit(solution)/shard_map/all_gather | solution.py:352
  (342 other events, 2885.5 us)
Sparse Core Ops, SparseCore 0:
  9.7 28.5 all-gather.5
  50.8 42.7 all-reduce.12
  95.4 26.3 all-gather.7
  146.6 45.6 all-reduce.22
  239.9 46.5 all-reduce.20
  341.2 44.1 all-reduce.18
  432.4 41.6 all-reduce.16
  501.4 43.6 all-reduce.14
  547.7 62.9 reduce-scatter.7
  612.9 61.9 reduce-scatter.13
  677.9 61.8 reduce-scatter.11
  742.7 61.8 reduce-scatter.15
  807.5 59.2 reduce-scatter.9
  868.5 31.8 all-gather.9
  902.0 33.9 all-gather.13
  937.7 33.9 all-gather.11
where the time goes:
time: 991 us; the launch traced here: 983 us
  waiting for transfers between devices  571 us (58%)
  matrix products  146 us (15%)
  other arithmetic  75.3 us (8%)
  local copies, waits for them, and re-layouts  71.8 us (7%)
  blocking collectives  71.4 us (7%)
  starting transfers between devices  27.5 us (3%)
  between operations  20 us (2%)
    reduce_scatter x4, waiting for transfers between devices, per_device(): lax.psum_scatter(as_sent(totals), 'dp', scatter_dimension=1, tiled=True)  188 us
    psum x5, waiting for transfers between devices, per_device(): lax.psum(d_hmlp.astype(jnp.bfloat16), 'tensor').astype(jnp.float32)  151 us
    all_gather x3, waiting for transfers between devices, per_device(): lax.all_gather(as_sent(totals), 'dp', axis=1, tiled=True)  74.9 us
    unnamed x17, waiting for transfers between devices  62.3 us
    dot_general x20, matrix products, contract_rows(): lax.dot_general(left, right, (((0,), (0,)), ((), ())), preferred_element_...  59.5 us
    unnamed x1, blocking collectives  53.1 us
    psum x1, waiting for transfers between devices, per_device(): lax.psum(partial_value.astype(jnp.bfloat16), 'tensor').astype(jnp.float32)  33.5 us
    unnamed x742, local copies, waits for them, and re-layouts  32.6 us
  transfers between devices with their start and end apart: 24, of which 20 were waited for; matrix products, arithmetic and copies ran while one was open for 14% of the time, Pallas kernels for 0%

commit v1 on v0

--- a/solution.py
+++ b/solution.py
@@ -126,10 +126,11 @@
     up_add = up_bias[0].astype(jnp.float32)
     down_mat = down_weight[0]
     bias_sum = output_bias[0, 0].astype(jnp.float32) + output_bias[0, 1].astype(jnp.float32)
-    input_rows, output_grads = (
-        lax.all_gather(tokens, "tensor", axis=1, tiled=True),
-        lax.all_gather(cotangent, "tensor", axis=1, tiled=True),
-    )
+    gathered_rows = lax.all_gather(
+        jnp.concatenate([tokens, cotangent], axis=0), "tensor", axis=1, tiled=True
+    )
+    input_rows = gathered_rows[: tokens.shape[0]]
+    output_grads = gathered_rows[tokens.shape[0] :]
     segment_all, place_all = positions(lengths, MB)
     cos_all, sin_all = rotary(place_all)
 
@@ -308,7 +309,7 @@
             [d_queries, d_keys, d_values.reshape(block_len, local_width)], axis=1
         )
         grad_joined_add = jnp.sum(d_joined.astype(jnp.float32), axis=0)
-        backward_grad_joined = contract_rows(h_attn, d_joined)
+        backward_grad_joined = contract_rows(d_joined, h_attn)
         d_hattn = contract_cols(d_joined, joined_mat)
         d_hattn, d_hmlp = (
             lax.psum(d_hattn.astype(jnp.bfloat16), "tensor").astype(jnp.float32),
@@ -343,25 +344,27 @@
             totals = jax.tree.map(lambda older, newer: older + newer, totals, terms)
         if section_tick < NMB:
             returned = passed_along(grad_low, "pipe", -1)
-    totals = jax.tree.map(
-        lambda part: part.astype(jnp.float32),
-        lax.psum_scatter(as_sent(totals), "dp", scatter_dimension=1, tiled=True),
-    )
-    summed = jax.tree.map(
-        lambda part, own: part.astype(own.dtype),
-        lax.all_gather(as_sent(totals), "dp", axis=1, tiled=True),
-        totals,
-    )
+    small_rows = totals[4][0]
+    small_pad = (-small_rows.shape[0]) % model_width
+    small_rows = jnp.pad(small_rows, (0, small_pad)).reshape(-1, model_width)
+    pieces = (totals[0][0], totals[1][0], totals[2][0], totals[3][0], small_rows)
+    slab = jnp.concatenate([piece.astype(jnp.bfloat16) for piece in pieces], axis=0)
+    slab = lax.psum(slab, "dp").astype(jnp.float32)
+    summed = []
+    offset = 0
+    for piece in pieces:
+        summed.append(slab[offset : offset + piece.shape[0]])
+        offset = offset + piece.shape[0]
     grad_rows_all = jnp.concatenate(
         [jnp.where(leading, tick_grads[block + 1], tick_grads[block]) for block in range(NMB)],
         axis=0,
     )
     input_grad = lax.dynamic_slice_in_dim(grad_rows_all, column_start, quarter, 1)[None]
-    grad_joined = summed[0].reshape(1, model_width, 3, local_width)
-    grad_dense = summed[1]
-    grad_up = summed[2]
-    grad_down = summed[3]
-    small_sum = summed[4][0]
+    grad_joined = summed[0].T.reshape(1, model_width, 3, local_width)
+    grad_dense = summed[1][None]
+    grad_up = summed[2][None]
+    grad_down = summed[3][None]
+    small_sum = summed[4].reshape(-1)
     offset = 0
     grad_ln_gain = small_sum[offset : offset + 2 * model_width].reshape(1, 2, model_width)
     offset = offset + 2 * model_width

time: 991 us -> 729 us (0.74)
  waiting for transfers between devices: 571 us -> 379 us
  blocking collectives: 71.4 us -> 0 us
  matrix products: 146 us -> 156 us
    reduce_scatter x4 -> x0, waiting for transfers between devices: 188 us -> none  [per_device(): lax.psum_scatter(as_sent(totals), 'dp', scatter_dimension=1, tiled=True)]
    psum x1 -> x5, waiting for transfers between devices: 33.5 us -> 170 us  [per_device(): lax.psum(partial_value.astype(jnp.bfloat16), 'tensor').astype(jnp.float32)]
    psum x0 -> x1, waiting for transfers between devices: none -> 134 us  [per_device(): slab = lax.psum(slab, 'dp').astype(jnp.float32)]
    psum x5 -> x1, waiting for transfers between devices: 151 us -> 40 us  [per_device(): lax.psum(d_hmlp.astype(jnp.bfloat16), 'tensor').astype(jnp.float32)]
    all_gather x5 -> x1, waiting for transfers between devices: 117 us -> 22.8 us  [per_device(): lax.all_gather(jnp.concatenate([tokens, cotangent], axis=0), 'tensor', ax...]
    unnamed x17 -> x8, waiting for transfers between devices: 62.3 us -> 0.13 us
    unnamed x1 -> x0, blocking collectives: 53.1 us -> none
    all_gather x1 -> x0, blocking collectives: 18.3 us -> none  [per_device(): lax.all_gather(as_sent(totals), 'dp', axis=1, tiled=True)]
  transfers between devices with their start and end apart: 24 -> 16, of which waited for: 20 -> 15; matrix products, arithmetic and copies ran while one was open for 14% -> 12% of each run, Pallas kernels for 0% -> 0%
where the time goes in v1:
time: 729 us; the launch traced here: 722 us
  waiting for transfers between devices  379 us (52%)
  matrix products  156 us (21%)
  other arithmetic  69 us (9%)
  local copies, waits for them, and re-layouts  68.6 us (9%)
  starting transfers between devices  30.2 us (4%)
  between operations  18.4 us (3%)
    psum x5, waiting for transfers between devices, per_device(): lax.psum(partial_value.astype(jnp.bfloat16), 'tensor').astype(jnp.float32)  170 us
    psum x1, waiting for transfers between devices, per_device(): slab = lax.psum(slab, 'dp').astype(jnp.float32)  134 us
    dot_general x20, matrix products, contract_rows(): lax.dot_general(left, right, (((0,), (0,)), ((), ())), preferred_element_...  68.6 us
    psum x1, waiting for transfers between devices, per_device(): lax.psum(d_hmlp.astype(jnp.bfloat16), 'tensor').astype(jnp.float32)  40 us
    dot_general x20, matrix products, contract_cols(): lax.dot_general(left, right, (((1,), (1,)), ((), ())), preferred_element_...  32.1 us
    ppermute x8, starting transfers between devices, passed_along(): return lax.ppermute(x, axis, pairs)  29.9 us
    all_gather x1, waiting for transfers between devices, per_device(): lax.all_gather(jnp.concatenate([tokens, cotangent], axis=0), 'tensor', ax...  22.8 us
    unnamed x619, local copies, waits for them, and re-layouts  20.6 us
  transfers between devices with their start and end apart: 16, of which 15 were waited for; matrix products, arithmetic and copies ran while one was open for 12% of the time, Pallas kernels for 0%

profile of v1, /device:TPU:0, one launch (start us, length us, event | category | flops | bytes accessed | tf_op | source)
XLA Modules:
  0.0 721.9 jit_solution(4068381418110488269)
XLA Ops:
  24.7 22.8 %all-gather.2.cloned.1.call-done = bf16[1024,1024]{1,0:T(8,128)(2,1)} async-done(((bf16[1024,256]{1,0:T(8,128)(2,1)}), bf16[1024,1024]{1,0:T(8,128)(2,1)}) %all-gather.2.cloned.1.call-update) | async-done | bytes 2097168 | tf_op jit(solution)/shard_map/all_gather | solution.py:129
  60.0 42.3 %all-reduce.14.cloned.1.call-done = bf16[128,1024]{1,0:T(8,128)(2,1)} async-done(((bf16[128,1024]{1,0:T(8,128)(2,1)}), bf16[128,1024]{1,0:T(8,128)(2,1)}) %all-reduce.14.cloned.1.call-update) | async-done | bytes 262160 | tf_op jit(solution)/shard_map/psum | solution.py:212
  103.4 5.4 collective-permute-start
  121.3 2.9 fusion.50
  131.7 3.6 convert_reduce_fusion.24
  138.2 3.9 fusion.386
  142.0 3.4 fusion.395
  146.2 5.4 fusion.377
  151.6 32.8 %all-reduce.26.cloned.1.call-done = (bf16[128,1024]{1,0:T(8,128)(2,1)}, bf16[128,1024]{1,0:T(8,128)(2,1)}, bf16[128,1024]{1,0:T(8,128)(2,1)}) async-done(((bf16[128,1024]{1,0:T(8,128)(2,1)}, bf16[128,1024]{1,0:T(8,128)(2,1)}, bf16[128,1024]{1,0:T(8,128)(2,1)}), (bf16[128,1024]{1,0:T(8,128)(2,1)}, bf16[128,1024]{1,0:T(8,128)(2,1)}, bf16[128,1024]{1,0:T(8,128)(2,1)})) %all-reduce.26.cloned.1.call-update) | async-done | bytes 786448 | tf_op jit(solution)/shard_map/psum | solution.py:212
  189.9 6.2 collective-permute-start.1
  212.3 2.9 fusion.53
  234.1 4.0 fusion.384
  238.2 3.5 fusion.393
  242.5 4.5 fusion.375
  246.9 34.4 %all-reduce.24.cloned.1.call-done = (bf16[128,1024]{1,0:T(8,128)(2,1)}, bf16[128,1024]{1,0:T(8,128)(2,1)}, bf16[128,1024]{1,0:T(8,128)(2,1)}) async-done(((bf16[128,1024]{1,0:T(8,128)(2,1)}, bf16[128,1024]{1,0:T(8,128)(2,1)}, bf16[128,1024]{1,0:T(8,128)(2,1)}), (bf16[128,1024]{1,0:T(8,128)(2,1)}, bf16[128,1024]{1,0:T(8,128)(2,1)}, bf16[128,1024]{1,0:T(8,128)(2,1)})) %all-reduce.24.cloned.1.call-update) | async-done | bytes 786448 | tf_op jit(solution)/shard_map/psum | solution.py:212
  287.5 6.3 collective-permute-start.2
  328.6 2.9 fusion.382
  335.4 3.3 fusion.391
  339.4 4.4 fusion.373
  343.8 38.7 %all-reduce.22.cloned.1.call-done = (bf16[128,1024]{1,0:T(8,128)(2,1)}, bf16[128,1024]{1,0:T(8,128)(2,1)}, bf16[128,1024]{1,0:T(8,128)(2,1)}) async-done(((bf16[128,1024]{1,0:T(8,128)(2,1)}, bf16[128,1024]{1,0:T(8,128)(2,1)}, bf16[128,1024]{1,0:T(8,128)(2,1)}), (bf16[128,1024]{1,0:T(8,128)(2,1)}, bf16[128,1024]{1,0:T(8,128)(2,1)}, bf16[128,1024]{1,0:T(8,128)(2,1)})) %all-reduce.22.cloned.1.call-update) | async-done | bytes 786448 | tf_op jit(solution)/shard_map/psum | solution.py:212
  388.2 6.5 collective-permute-start.3
  428.0 4.0 fusion.380
  432.0 4.4 fusion.371
  445.3 40.0 %all-reduce.20.cloned.1.call-done = (bf16[128,1024]{1,0:T(8,128)(2,1)}, bf16[128,1024]{1,0:T(8,128)(2,1)}) async-done(((bf16[128,1024]{1,0:T(8,128)(2,1)}, bf16[128,1024]{1,0:T(8,128)(2,1)}), (bf16[128,1024]{1,0:T(8,128)(2,1)}, bf16[128,1024]{1,0:T(8,128)(2,1)})) %all-reduce.20.cloned.1.call-update) | async-done | bytes 524304 | tf_op jit(solution)/shard_map/psum | solution.py:316
  511.5 6.9 fusion.42
  527.4 6.8 fusion
  534.3 21.9 %all-reduce.18.cloned.1.call-done = (bf16[128,1024]{1,0:T(8,128)(2,1)}, bf16[128,1024]{1,0:T(8,128)(2,1)}, bf16[128,1024]{1,0:T(8,128)(2,1)}) async-done(((bf16[128,1024]{1,0:T(8,128)(2,1)}, bf16[128,1024]{1,0:T(8,128)(2,1)}, bf16[128,1024]{1,0:T(8,128)(2,1)}), (bf16[128,1024]{1,0:T(8,128)(2,1)}, bf16[128,1024]{1,0:T(8,128)(2,1)}, bf16[128,1024]{1,0:T(8,128)(2,1)})) %all-reduce.18.cloned.1.call-update) | async-done | bytes 786448 | tf_op jit(solution)/shard_map/psum | solution.py:212
  562.9 133.6 %all-reduce.16.cloned.1.call-done = bf16[3080,1024]{1,0:T(8,128)(2,1)} async-done(((bf16[3080,1024]{1,0:T(8,128)(2,1)}), bf16[3080,1024]{1,0:T(8,128)(2,1)}) %all-reduce.16.cloned.1.call-update) | async-done | bytes 6307856 | tf_op jit(solution)/shard_map/psum | solution.py:352
  696.4 4.3 convert_element_type.684
  702.4 4.2 slice_bitcast_fusion
  707.3 3.4 slice.631
  710.7 3.5 copy.182
  (908 shorter events, 230.2 us)
Async XLA Ops:
  7.2 49.9 %copy-start = (bf16[1,1024,1024]{2,1,0:T(8,128)(2,1)S(1)}, bf16[1,1024,1024]{2,1,0:T(8,128)(2,1)}, u32[]{:S(2)}) copy-start(bf16[1,1024,1024]{2,1,0:T(8,128)(2,1)} %param.21) | copy-start | bytes 6291460
  7.2 40.3 %all-gather.2.cloned.1.call-start = ((), (), s32[]{:S(2)}) async-start(), calls=%async_computation | async-start | bytes 2621440 | tf_op jit(solution)/shard_map/all_gather | solution.py:129
  9.3 93.0 %all-reduce.14.cloned.1.call-start = ((), (), s32[]{:S(2)}) async-start(), calls=%async_computation.1 | async-start | bytes 524288 | tf_op jit(solution)/shard_map/psum | solution.py:212
  57.1 51.7 %copy-start.281 = (s32[128]{0:T(128)S(1)}, s32[128]{0:T(128)}, u32[]{:S(2)}) copy-start(s32[128]{0:T(128)} %get-tuple-element.106) | copy-start | bytes 1540
  57.1 51.7 %copy-start.282 = (s32[128]{0:T(128)S(1)}, s32[128]{0:T(128)}, u32[]{:S(2)}) copy-start(s32[128]{0:T(128)} %get-tuple-element.246) | copy-start | bytes 1540
  59.3 125.1 %all-reduce.26.cloned.1.call-start = ((), (), s32[]{:S(2)}) async-start(), calls=%async_computation.7 | async-start | bytes 1572864 | tf_op jit(solution)/shard_map/psum | solution.py:212
  59.4 50.1 %copy-start.90 = (f32[1,1,1024]{2,1,0:T(1,128)}, f32[1,1,1024]{2,1,0:T(1,128)S(1)}, u32[]{:S(2)}) copy-start(f32[1,1,1024]{2,1,0:T(1,128)S(1)} %convert_add_fusion.10) | copy-start | bytes 12292
  103.4 8.8 %collective-permute-start = (bf16[128,1024]{1,0:T(8,128)(2,1)S(1)}, bf16[128,1024]{1,0:T(8,128)(2,1)S(1)}, u32[]{:S(2)}, u32[]{:S(2)}) collective-permute-start(bf16[128,1024]{1,0:T(8,128)(2,1)S(1)} %fusion.193), channel_id=1, source_target_pairs={{0,64},{1,65},{2,66},{3,67},{4,68},{5,69},{6,70},{7,71},{8,72},{9,... | collective-permute-start | bytes 786440 | tf_op jit(solution)/shard_map/ppermute | solution.py:19
  138.1 143.2 %all-reduce.24.cloned.1.call-start = ((), (), s32[]{:S(2)}) async-start(), calls=%async_computation.6 | async-start | bytes 1572864 | tf_op jit(solution)/shard_map/psum | solution.py:212
  146.2 40.0 %copy-start.279 = (f32[128]{0:T(128)S(1)}, f32[128]{0:T(128)}, u32[]{:S(2)}) copy-start(f32[128]{0:T(128)} %get-tuple-element.267) | copy-start | bytes 1540
  187.7 9.8 %collective-permute-start.4 = (bf16[128,1024]{1,0:T(8,128)(2,1)S(1)}, bf16[128,1024]{1,0:T(8,128)(2,1)S(1)}, u32[]{:S(2)}, u32[]{:S(2)}) collective-permute-start(bf16[128,1024]{1,0:T(8,128)(2,1)S(1)} %fusion.187), channel_id=1, source_target_pairs={{64,0},{65,1},{66,2},{67,3},{68,4},{69,5},{70,6},{71,7},{72,8},{73... | collective-permute-start | bytes 786440 | tf_op jit(solution)/shard_map/ppermute | solution.py:19
  189.9 9.9 %collective-permute-start.1 = (bf16[128,1024]{1,0:T(8,128)(2,1)S(1)}, bf16[128,1024]{1,0:T(8,128)(2,1)S(1)}, u32[]{:S(2)}, u32[]{:S(2)}) collective-permute-start(bf16[128,1024]{1,0:T(8,128)(2,1)S(1)} %get-tuple-element.133), channel_id=1, source_target_pairs={{0,64},{1,65},{2,66},{3,67},{4,68},{5,69},{6,70},{7,71},{8,72},{9,... | collective-permute-start | bytes 786440 | tf_op jit(solution)/shard_map/ppermute | solution.py:19
  201.7 81.5 %copy-start.21 = (bf16[128,1024]{1,0:T(8,128)(2,1)}, bf16[128,1024]{1,0:T(8,128)(2,1)S(1)}, u32[]{:S(2)}) copy-start(bf16[128,1024]{1,0:T(8,128)(2,1)S(1)} %get-tuple-element.91) | copy-start | bytes 786436
  234.0 148.5 %all-reduce.22.cloned.1.call-start = ((), (), s32[]{:S(2)}) async-start(), calls=%async_computation.5 | async-start | bytes 1572864 | tf_op jit(solution)/shard_map/psum | solution.py:212
  242.4 38.9 %copy-start.190 = (f32[128]{0:T(128)S(1)}, f32[128]{0:T(128)}, u32[]{:S(2)}) copy-start(f32[128]{0:T(128)} %copy-done.186) | copy-start | bytes 1540
  242.5 38.9 %copy-start.205 = (f32[128]{0:T(128)S(1)}, f32[128]{0:T(128)}, u32[]{:S(2)}) copy-start(f32[128]{0:T(128)} %copy-done.201) | copy-start | bytes 1540
  242.5 40.7 %copy-start.278 = (f32[128]{0:T(128)S(1)}, f32[128]{0:T(128)}, u32[]{:S(2)}) copy-start(f32[128]{0:T(128)} %get-tuple-element.265) | copy-start | bytes 1540
  246.9 39.7 %copy-start.92 = (f32[1,1,1024]{2,1,0:T(1,128)S(1)}, f32[1,1,1024]{2,1,0:T(1,128)}, u32[]{:S(2)}) copy-start(f32[1,1,1024]{2,1,0:T(1,128)} %copy-done.90) | copy-start | bytes 12292
  285.2 10.1 %collective-permute-start.5 = (bf16[128,1024]{1,0:T(8,128)(2,1)S(1)}, bf16[128,1024]{1,0:T(8,128)(2,1)S(1)}, u32[]{:S(2)}, u32[]{:S(2)}) collective-permute-start(bf16[128,1024]{1,0:T(8,128)(2,1)S(1)} %get-tuple-element.101), channel_id=1, source_target_pairs={{64,0},{65,1},{66,2},{67,3},{68,4},{69,5},{70,6},{71,7},{72,8},{73... | collective-permute-start | bytes 786440 | tf_op jit(solution)/shard_map/ppermute | solution.py:19
  287.5 9.9 %collective-permute-start.2 = (bf16[128,1024]{1,0:T(8,128)(2,1)S(1)}, bf16[128,1024]{1,0:T(8,128)(2,1)S(1)}, u32[]{:S(2)}, u32[]{:S(2)}) collective-permute-start(bf16[128,1024]{1,0:T(8,128)(2,1)S(1)} %get-tuple-element.128), channel_id=1, source_target_pairs={{0,64},{1,65},{2,66},{3,67},{4,68},{5,69},{6,70},{7,71},{8,72},{9,... | collective-permute-start | bytes 786440 | tf_op jit(solution)/shard_map/ppermute | solution.py:19
  335.3 150.0 %all-reduce.20.cloned.1.call-start = ((), (), s32[]{:S(2)}) async-start(), calls=%async_computation.4 | async-start | bytes 1048576 | tf_op jit(solution)/shard_map/psum | solution.py:316
  339.4 43.2 %copy-start.118 = (f32[128]{0:T(128)S(1)}, f32[128]{0:T(128)}, u32[]{:S(2)}) copy-start(f32[128]{0:T(128)} %copy-done.116) | copy-start | bytes 1540
  339.4 43.2 %copy-start.122 = (f32[128]{0:T(128)S(1)}, f32[128]{0:T(128)}, u32[]{:S(2)}) copy-start(f32[128]{0:T(128)} %copy-done.120) | copy-start | bytes 1540
  339.4 43.1 %copy-start.134 = (f32[128]{0:T(128)S(1)}, f32[128]{0:T(128)}, u32[]{:S(2)}) copy-start(f32[128]{0:T(128)} %copy-done.130) | copy-start | bytes 1540
  339.4 43.1 %copy-start.139 = (f32[128]{0:T(128)S(1)}, f32[128]{0:T(128)}, u32[]{:S(2)}) copy-start(f32[128]{0:T(128)} %copy-done.135) | copy-start | bytes 1540
  339.4 44.7 %copy-start.93 = (f32[1,1,1024]{2,1,0:T(1,128)S(1)}, f32[1,1,1024]{2,1,0:T(1,128)}, u32[]{:S(2)}) copy-start(f32[1,1,1024]{2,1,0:T(1,128)} %copy-done.90) | copy-start | bytes 12292
  339.4 44.7 %copy-start.277 = (f32[128]{0:T(128)S(1)}, f32[128]{0:T(128)}, u32[]{:S(2)}) copy-start(f32[128]{0:T(128)} %get-tuple-element.263) | copy-start | bytes 1540
  386.9 9.8 %collective-permute-start.6 = (bf16[128,1024]{1,0:T(8,128)(2,1)S(1)}, bf16[128,1024]{1,0:T(8,128)(2,1)S(1)}, u32[]{:S(2)}, u32[]{:S(2)}) collective-permute-start(bf16[128,1024]{1,0:T(8,128)(2,1)S(1)} %get-tuple-element.99), channel_id=1, source_target_pairs={{64,0},{65,1},{66,2},{67,3},{68,4},{69,5},{70,6},{71,7},{72,8},{73... | collective-permute-start | bytes 786440 | tf_op jit(solution)/shard_map/ppermute | solution.py:19
  388.2 9.9 %collective-permute-start.3 = (bf16[128,1024]{1,0:T(8,128)(2,1)S(1)}, bf16[128,1024]{1,0:T(8,128)(2,1)S(1)}, u32[]{:S(2)}, u32[]{:S(2)}) collective-permute-start(bf16[128,1024]{1,0:T(8,128)(2,1)S(1)} %get-tuple-element.160), channel_id=1, source_target_pairs={{0,64},{1,65},{2,66},{3,67},{4,68},{5,69},{6,70},{7,71},{8,72},{9,... | collective-permute-start | bytes 786440 | tf_op jit(solution)/shard_map/ppermute | solution.py:19
  439.5 116.7 %all-reduce.18.cloned.1.call-start = ((), (), s32[]{:S(2)}) async-start(), calls=%async_computation.3 | async-start | bytes 1572864 | tf_op jit(solution)/shard_map/psum | solution.py:212
  489.2 9.9 %collective-permute-start.7 = (bf16[128,1024]{1,0:T(8,128)(2,1)S(1)}, bf16[128,1024]{1,0:T(8,128)(2,1)S(1)}, u32[]{:S(2)}, u32[]{:S(2)}) collective-permute-start(bf16[128,1024]{1,0:T(8,128)(2,1)S(1)} %get-tuple-element.97), channel_id=1, source_target_pairs={{64,0},{65,1},{66,2},{67,3},{68,4},{69,5},{70,6},{71,7},{72,8},{73... | collective-permute-start | bytes 786440 | tf_op jit(solution)/shard_map/ppermute | solution.py:19
  511.3 185.1 %all-reduce.16.cloned.1.call-start = ((), (), s32[]{:S(2)}) async-start(), calls=%async_computation.2 | async-start | bytes 12615680 | tf_op jit(solution)/shard_map/psum | solution.py:352
  (274 other events, 2010.6 us)
Sparse Core Ops, SparseCore 0:
  10.3 37.2 all-gather.1
  59.4 42.7 all-reduce.13
  138.2 46.1 all-reduce.25
  234.2 47.1 all-reduce.23
  335.4 47.1 all-reduce.21
  439.6 45.6 all-reduce.19
  511.4 44.6 all-reduce.17
  559.5 136.9 all-reduce.15
